TPU v7x, 512 devices: a whole 4x8x8 slice. The times are simulated.
512 devices in a mesh: expert: 32 (over y, z_lo, core), tensor: 16 (over x, z_hi).
Axes of the slice: x: 4, y: 8, z: 8 (z_hi: 4, z_lo: 2; z = z_hi * 2 + z_lo), core: 2. Of those that a mesh axis runs over, the one named last changes fastest.
Arguments:
- tokens: bfloat16 [4096, 6144], P('expert', 'tensor'), may hold values from -6 to 6
- expert_ids: int32 [4096, 2], P('expert'), may hold values from 0 to 7, all different within a row; in each aligned block of 128 rows (0 to 127, 128 to 255, ...) at most 48 rows name the same one
- gate_fixed: int32 [4096, 2], P('expert'), may hold values from 4096 to 65535
- w_gate: bfloat16 [32, 1024, 6144], P('expert', None, 'tensor'), may hold values from -0.078125 to 0.078125
- w_up: bfloat16 [32, 1024, 6144], P('expert', None, 'tensor'), may hold values from -0.078125 to 0.078125
- w_down: bfloat16 [32, 1024, 6144], P('expert', None, 'tensor'), may hold values from -0.0625 to 0.0625
Outputs:
- mixed: bfloat16 [4096, 6144], P('expert', 'tensor')
Inputs may be any that keep to these rules, and one draw needn't show every extreme that they name: `expert_ids`: each row names 2 different experts. Among the 128 rows of one sequence shard (aligned blocks), no expert is named by more than 48 rows, a bound that some block reaches.
All inputs are finite; a program needn't handle non-finite values.
Results may differ from a plain program's by a relative error of at most 0.0064.
Values may be sent and summed in bfloat16 or wider, within the bound.
No kernel may reach another device: no remote copies, remote signals or barrier semaphores. Data moves between devices by JAX's collectives and lax.ppermute only.
A program may use at most 64 MiB of HBM per device.

v0:
```python
import jax
import jax.numpy as jnp
from jax import lax
from jax.sharding import PartitionSpec as P

EXPERTS = 4
CAP = 48


def on_device(tokens, expert_ids, gate_fixed, w_gate, w_up, w_down):
    width_part = tokens.shape[1]
    quarters = lax.axis_size("expert") // EXPERTS
    groups = lax.axis_size("tensor")
    expert_iota = jnp.arange(EXPERTS, dtype=jnp.int32)
    matched = expert_ids[:, :, None] == expert_iota
    routed = jnp.sum(matched.astype(jnp.int32), axis=1)
    weights = (
        jnp.sum(jnp.where(matched, gate_fixed[:, :, None], 0), axis=1).astype(jnp.float32) / 65536.0
    )
    position = jnp.cumsum(routed, axis=0) - routed
    slot_iota = jnp.arange(CAP, dtype=jnp.int32)
    placed = (position[:, :, None] == slot_iota) & (routed[:, :, None] > 0)
    outgoing = jnp.einsum(
        "tec,td->ecd", placed.astype(jnp.bfloat16), tokens, preferred_element_type=jnp.float32
    ).astype(jnp.bfloat16)
    outgoing = jnp.tile(outgoing, (quarters, 1, 1))
    arrived = lax.all_to_all(outgoing, "expert", split_axis=0, concat_axis=0, tiled=True)
    sources = arrived.shape[0]
    total_rows = sources * CAP
    rows_in = arrived.reshape(total_rows, width_part)
    gate_local = w_gate[0]
    up_local = w_up[0]
    down_local = w_down[0]
    hidden_width = gate_local.shape[0]
    contract = (((1,), (1,)), ((), ()))
    gate_term = lax.dot_general(
        rows_in, gate_local, contract, preferred_element_type=jnp.float32
    ).astype(jnp.bfloat16)
    up_term = lax.dot_general(
        rows_in, up_local, contract, preferred_element_type=jnp.float32
    ).astype(jnp.bfloat16)
    gate_parts, up_parts = (
        lax.all_to_all(gate_term, "tensor", split_axis=0, concat_axis=0, tiled=True),
        lax.all_to_all(up_term, "tensor", split_axis=0, concat_axis=0, tiled=True),
    )
    row_share = total_rows // groups
    gate_share = jnp.sum(
        gate_parts.reshape(groups, row_share, hidden_width).astype(jnp.float32), axis=0
    )
    up_share = jnp.sum(
        up_parts.reshape(groups, row_share, hidden_width).astype(jnp.float32), axis=0
    )
    hidden = (jax.nn.silu(gate_share) * up_share).astype(jnp.bfloat16)
    partial_out = jnp.dot(
        lax.all_gather(hidden, "tensor", axis=0, tiled=True),
        down_local,
        preferred_element_type=jnp.float32,
    )
    returned = lax.all_to_all(
        partial_out.reshape(sources, CAP, width_part),
        "expert",
        split_axis=0,
        concat_axis=0,
        tiled=True,
    )
    summed = jnp.sum(returned.reshape(quarters, EXPERTS, CAP, width_part), axis=0)
    selector = placed.astype(jnp.float32) * weights[:, :, None]
    mixed = jnp.einsum("tec,ecd->td", selector, summed, precision=lax.Precision.HIGHEST)
    return mixed.astype(jnp.bfloat16)


def solution(mesh):
    placed = (
        P("expert", "tensor"),
        P("expert", None),
        P("expert", None),
        P("expert", None, "tensor"),
        P("expert", None, "tensor"),
        P("expert", None, "tensor"),
    )
    return jax.shard_map(
        on_device, mesh=mesh, in_specs=placed, out_specs=P("expert", "tensor"), check_vma=False
    )
```

profile of v0, /device:TPU:1, one launch (start us, length us, event | category | flops | bytes accessed | tf_op | source)
XLA Modules:
  0.0 371.3 jit_solution(15921568439732790219)
XLA Ops:
  6.5 0.0 copy-start
  6.5 0.8 select_reduce_fusion
  7.3 0.1 copy.11
  7.4 0.2 reduce_window_sum.11
  7.6 0.1 copy.13
  7.7 1.1 convolution_convert_fusion.2
  8.8 0.1 tile.4
  8.9 41.6 %all_to_all.28 = bf16[32,48,384]{2,1,0:T(8,128)(2,1)S(1)} all-to-all(bf16[32,48,384]{2,1,0:T(8,128)(2,1)S(1)} %bitcast.28), channel_id=1, replica_groups=mesh['expert'=32,'tensor'=16] {'expert'}, dimensions={0} | all-to-all | bytes 2359296 | tf_op jit(solution)/shard_map/all_to_all | solution.py:27
  50.5 0.0 copy-done
  50.5 3.5 convolution_convert_fusion
  54.1 0.0 copy-start.1
  54.1 11.9 %all-to-all-start.2 = ((bf16[16,96,1024]{2,1,0:T(8,128)(2,1)}), bf16[16,96,1024]{2,1,0:T(8,128)(2,1)}, u32[]{:S(2)}, u32[]{:S(2)}) async-start(bf16[16,96,1024]{2,1,0:T(8,128)(2,1)} %bitcast.30), calls=%async_computation.2 | async-start | bytes 6291456 | tf_op jit(solution)/shard_map/all_to_all | solution.py:44
  66.0 0.0 copy-done.1
  66.0 3.5 convolution_convert_fusion.1
  69.5 58.6 %all-to-all-done.2 = bf16[16,96,1024]{2,1,0:T(8,128)(2,1)} async-done(((bf16[16,96,1024]{2,1,0:T(8,128)(2,1)}), bf16[16,96,1024]{2,1,0:T(8,128)(2,1)}, u32[]{:S(2)}, u32[]{:S(2)}) %all-to-all-start.2) | async-done | bytes 3145760 | tf_op jit(solution)/shard_map/all_to_all | solution.py:44
  128.1 16.4 %all-to-all-start.1 = ((bf16[16,96,1024]{2,1,0:T(8,128)(2,1)}), bf16[16,96,1024]{2,1,0:T(8,128)(2,1)}, u32[]{:S(2)}, u32[]{:S(2)}) async-start(bf16[16,96,1024]{2,1,0:T(8,128)(2,1)} %bitcast.29), calls=%async_computation.1 | async-start | bytes 6291456 | tf_op jit(solution)/shard_map/all_to_all | solution.py:43
  144.5 0.0 all-gather.2.cloned.1.call-start
  144.6 2.6 convert_reduce_fusion
  147.2 0.0 copy-start.2
  147.2 54.5 %all-to-all-done.1 = bf16[16,96,1024]{2,1,0:T(8,128)(2,1)} async-done(((bf16[16,96,1024]{2,1,0:T(8,128)(2,1)}), bf16[16,96,1024]{2,1,0:T(8,128)(2,1)}, u32[]{:S(2)}, u32[]{:S(2)}) %all-to-all-start.1) | async-done | bytes 3145760 | tf_op jit(solution)/shard_map/all_to_all | solution.py:43
  201.6 2.6 convert_reduce_fusion.1
  204.2 0.8 multiply_convert_fusion
  205.0 0.0 all-gather.2.cloned.1.call-update
  205.0 89.8 %all-gather.2.cloned.1.call-done = bf16[1536,1024]{1,0:T(8,128)(2,1)} async-done(((bf16[96,1024]{1,0:T(8,128)(2,1)}), bf16[1536,1024]{1,0:T(8,128)(2,1)}) %all-gather.2.cloned.1.call-update) | async-done | bytes 3145744 | tf_op jit(solution)/shard_map/all_gather | solution.py:55
  294.8 0.0 copy-done.2
  294.8 5.1 %fusion.1 = f32[32,48,384]{2,1,0:T(8,128)} fusion(bf16[32,48,1024]{2,1,0:T(8,128)(2,1)} %bitcast.33, bf16[1,1024,384]{2,1,0:T(8,128)(2,1)S(1)} %copy-done.2), kind=kOutput, calls=%fused_computation.7 | convolution fusion | flops 1207959552 | bytes 6291456 | tf_op jit(solution)/shard_map/dot_general | solution.py:54
  300.0 7.8 %all-to-all-start.3 = ((f32[32,48,384]{2,1,0:T(8,128)}), f32[32,48,384]{2,1,0:T(8,128)S(1)}, u32[]{:S(2)}, u32[]{:S(2)}) async-start(f32[32,48,384]{2,1,0:T(8,128)} %fusion.1), calls=%async_computation.3 | async-start | bytes 4718592 | tf_op jit(solution)/shard_map/all_to_all | solution.py:59
  307.8 55.5 %all-to-all-done.3 = f32[32,48,384]{2,1,0:T(8,128)S(1)} async-done(((f32[32,48,384]{2,1,0:T(8,128)}), f32[32,48,384]{2,1,0:T(8,128)S(1)}, u32[]{:S(2)}, u32[]{:S(2)}) %all-to-all-start.3) | async-done | bytes 2359328 | tf_op jit(solution)/shard_map/all_to_all | solution.py:59
  363.3 0.1 reduce_sum.49
  363.4 1.1 fusion
  (3 shorter events, 0.0 us)
Async XLA Ops:
  6.5 44.0 %copy-start = (bf16[1,1024,384]{2,1,0:T(8,128)(2,1)S(1)}, bf16[1,1024,384]{2,1,0:T(8,128)(2,1)}, u32[]{:S(2)}) copy-start(bf16[1,1024,384]{2,1,0:T(8,128)(2,1)} %param.10) | copy-start | bytes 2359300
  54.1 11.9 %copy-start.1 = (bf16[1,1024,384]{2,1,0:T(8,128)(2,1)S(1)}, bf16[1,1024,384]{2,1,0:T(8,128)(2,1)}, u32[]{:S(2)}) copy-start(bf16[1,1024,384]{2,1,0:T(8,128)(2,1)} %param.9) | copy-start | bytes 2359300
  54.1 74.1 %all-to-all-start.2 = ((bf16[16,96,1024]{2,1,0:T(8,128)(2,1)}), bf16[16,96,1024]{2,1,0:T(8,128)(2,1)}, u32[]{:S(2)}, u32[]{:S(2)}) async-start(bf16[16,96,1024]{2,1,0:T(8,128)(2,1)} %bitcast.30), calls=%async_computation.2 | async-start | bytes 6291456 | tf_op jit(solution)/shard_map/all_to_all | solution.py:44
  128.1 73.5 %all-to-all-start.1 = ((bf16[16,96,1024]{2,1,0:T(8,128)(2,1)}), bf16[16,96,1024]{2,1,0:T(8,128)(2,1)}, u32[]{:S(2)}, u32[]{:S(2)}) async-start(bf16[16,96,1024]{2,1,0:T(8,128)(2,1)} %bitcast.29), calls=%async_computation.1 | async-start | bytes 6291456 | tf_op jit(solution)/shard_map/all_to_all | solution.py:43
  144.5 150.3 %all-gather.2.cloned.1.call-start = ((), (), s32[]{:S(2)}) async-start(), calls=%async_computation.4 | async-start | bytes 3342336 | tf_op jit(solution)/shard_map/all_gather | solution.py:55
  147.2 147.7 %copy-start.2 = (bf16[1,1024,384]{2,1,0:T(8,128)(2,1)S(1)}, bf16[1,1024,384]{2,1,0:T(8,128)(2,1)}, u32[]{:S(2)}) copy-start(bf16[1,1024,384]{2,1,0:T(8,128)(2,1)} %param.11) | copy-start | bytes 2359300
  300.0 63.3 %all-to-all-start.3 = ((f32[32,48,384]{2,1,0:T(8,128)}), f32[32,48,384]{2,1,0:T(8,128)S(1)}, u32[]{:S(2)}, u32[]{:S(2)}) async-start(f32[32,48,384]{2,1,0:T(8,128)} %fusion.1), calls=%async_computation.3 | async-start | bytes 4718592 | tf_op jit(solution)/shard_map/all_to_all | solution.py:59
Sparse Core Ops, SparseCore 0:
  205.2 89.6 all-gather.1
where the time goes:
time: 372 us; the launch traced here: 371 us
  waiting for transfers between devices  258 us (69%)
  blocking collectives  41.6 us (11%)
  starting transfers between devices  36.1 us (10%)
  matrix products  14.4 us (4%)
  between operations  13.5 us (4%)
  other arithmetic  7.05 us (2%)
    all_gather x1, waiting for transfers between devices, on_device(): lax.all_gather(hidden, 'tensor', axis=0, tiled=True)  89.8 us
    all_to_all x1, waiting for transfers between devices, on_device(): lax.all_to_all(up_term, 'tensor', split_axis=0, concat_axis=0, tiled=True)  58.6 us
    all_to_all x1, waiting for transfers between devices, on_device(): lax.all_to_all(partial_out.reshape(sources, CAP, width_part), 'expert', s...  55.5 us
    all_to_all x1, waiting for transfers between devices, on_device(): lax.all_to_all(gate_term, 'tensor', split_axis=0, concat_axis=0, tiled=True)  54.5 us
    all_to_all x1, blocking collectives, on_device(): lax.all_to_all(outgoing, 'expert', split_axis=0, concat_axis=0, tiled=True)  41.6 us
    all_to_all x1, starting transfers between devices, on_device(): lax.all_to_all(gate_term, 'tensor', split_axis=0, concat_axis=0, tiled=True)  16.4 us
    all_to_all x1, starting transfers between devices, on_device(): lax.all_to_all(up_term, 'tensor', split_axis=0, concat_axis=0, tiled=True)  11.9 us
    all_to_all x1, starting transfers between devices, on_device(): lax.all_to_all(partial_out.reshape(sources, CAP, width_part), 'expert', s...  7.78 us
  transfers between devices with their start and end apart: 4, of which 4 were waited for; matrix products, arithmetic and copies ran while one was open for 2% of the time, Pallas kernels for 0%

commit v1 on v0

--- a/solution.py
+++ b/solution.py
@@ -5,6 +5,13 @@
 
 EXPERTS = 4
 CAP = 48
+
+
+def gather_over(value, axis, dim):
+    count = lax.axis_size(axis)
+    blocks = jnp.stack([value for _ in range(count)])
+    blocks = lax.all_to_all(blocks, axis, split_axis=0, concat_axis=0)
+    return jnp.concatenate(blocks, axis=dim)
 
 
 def on_device(tokens, expert_ids, gate_fixed, w_gate, w_up, w_down):
@@ -52,9 +59,7 @@
     )
     hidden = (jax.nn.silu(gate_share) * up_share).astype(jnp.bfloat16)
     partial_out = jnp.dot(
-        lax.all_gather(hidden, "tensor", axis=0, tiled=True),
-        down_local,
-        preferred_element_type=jnp.float32,
+        gather_over(hidden, "tensor", 0), down_local, preferred_element_type=jnp.float32
     )
     returned = lax.all_to_all(
         partial_out.reshape(sources, CAP, width_part),

time: 372 us -> 359 us (0.965)
  waiting for transfers between devices: 258 us -> 169 us
  blocking collectives: 41.6 us -> 121 us
  between operations: 13.5 us -> 0.1 us
  starting transfers between devices: 36.1 us -> 49.3 us
    all_gather x1 -> x0, waiting for transfers between devices: 89.8 us -> none  [on_device(): lax.all_gather(hidden, 'tensor', axis=0, tiled=True)]
    all_to_all x0 -> x1, blocking collectives: none -> 79.5 us  [gather_over(): blocks = lax.all_to_all(blocks, axis, split_axis=0, concat_axis=0)]
    all_to_all x1, starting transfers between devices: 7.78 us -> 21 us  [on_device(): lax.all_to_all(partial_out.reshape(sources, CAP, width_part), 'expert', s...]
  transfers between devices with their start and end apart: 4 -> 3, of which waited for: 4 -> 3; matrix products, arithmetic and copies ran while one was open for 2% -> 2% of each run, Pallas kernels for 0% -> 0%
where the time goes in v1:
time: 359 us
  waiting for transfers between devices  169 us (47%)
  blocking collectives  121 us (34%)
  starting transfers between devices  49.3 us (14%)
  matrix products  12.5 us (3%)
  other arithmetic  6.36 us (2%)
    all_to_all x1, blocking collectives, gather_over(): blocks = lax.all_to_all(blocks, axis, split_axis=0, concat_axis=0)  79.5 us
    all_to_all x1, waiting for transfers between devices, on_device(): lax.all_to_all(up_term, 'tensor', split_axis=0, concat_axis=0, tiled=True)  58.6 us
    all_to_all x1, waiting for transfers between devices, on_device(): lax.all_to_all(partial_out.reshape(sources, CAP, width_part), 'expert', s...  55.5 us
    all_to_all x1, waiting for transfers between devices, on_device(): lax.all_to_all(gate_term, 'tensor', split_axis=0, concat_axis=0, tiled=True)  54.5 us
    all_to_all x1, blocking collectives, on_device(): lax.all_to_all(outgoing, 'expert', split_axis=0, concat_axis=0, tiled=True)  41.6 us
    all_to_all x1, starting transfers between devices, on_device(): lax.all_to_all(partial_out.reshape(sources, CAP, width_part), 'expert', s...  21 us
    all_to_all x1, starting transfers between devices, on_device(): lax.all_to_all(gate_term, 'tensor', split_axis=0, concat_axis=0, tiled=True)  16.4 us
    all_to_all x1, starting transfers between devices, on_device(): lax.all_to_all(up_term, 'tensor', split_axis=0, concat_axis=0, tiled=True)  11.9 us
  transfers between devices with their start and end apart: 3, of which 3 were waited for; matrix products, arithmetic and copies ran while one was open for 2% of the time, Pallas kernels for 0%

profile of v1, /device:TPU:1, one launch (start us, length us, event | category | flops | bytes accessed | tf_op | source)
XLA Modules:
  0.0 358.6 jit_solution(17424086133381151937)
XLA Ops:
  0.0 0.0 copy-start
  0.0 0.8 select_reduce_fusion
  0.8 0.1 copy.11
  0.9 0.2 reduce_window_sum.11
  1.1 0.1 copy.13
  1.1 1.1 convolution_convert_fusion.2
  2.3 0.1 tile.4
  2.4 41.6 %all_to_all.33 = bf16[32,48,384]{2,1,0:T(8,128)(2,1)S(1)} all-to-all(bf16[32,48,384]{2,1,0:T(8,128)(2,1)S(1)} %bitcast.28), channel_id=1, replica_groups=mesh['expert'=32,'tensor'=16] {'expert'}, dimensions={0} | all-to-all | bytes 2359296 | tf_op jit(solution)/shard_map/all_to_all | solution.py:34
  44.0 0.0 copy-done
  44.0 3.5 convolution_convert_fusion
  47.5 0.0 copy-start.1
  47.5 11.9 %all-to-all-start.2 = ((bf16[16,96,1024]{2,1,0:T(8,128)(2,1)}), bf16[16,96,1024]{2,1,0:T(8,128)(2,1)}, u32[]{:S(2)}, u32[]{:S(2)}) async-start(bf16[16,96,1024]{2,1,0:T(8,128)(2,1)} %bitcast.30), calls=%async_computation.2 | async-start | bytes 6291456 | tf_op jit(solution)/shard_map/all_to_all | solution.py:51
  59.4 0.0 copy-done.1
  59.4 3.5 convolution_convert_fusion.1
  63.0 58.6 %all-to-all-done.2 = bf16[16,96,1024]{2,1,0:T(8,128)(2,1)} async-done(((bf16[16,96,1024]{2,1,0:T(8,128)(2,1)}), bf16[16,96,1024]{2,1,0:T(8,128)(2,1)}, u32[]{:S(2)}, u32[]{:S(2)}) %all-to-all-start.2) | async-done | bytes 3145760 | tf_op jit(solution)/shard_map/all_to_all | solution.py:51
  121.6 16.4 %all-to-all-start.1 = ((bf16[16,96,1024]{2,1,0:T(8,128)(2,1)}), bf16[16,96,1024]{2,1,0:T(8,128)(2,1)}, u32[]{:S(2)}, u32[]{:S(2)}) async-start(bf16[16,96,1024]{2,1,0:T(8,128)(2,1)} %bitcast.29), calls=%async_computation.1 | async-start | bytes 6291456 | tf_op jit(solution)/shard_map/all_to_all | solution.py:50
  138.0 2.6 convert_reduce_fusion
  140.6 54.5 %all-to-all-done.1 = bf16[16,96,1024]{2,1,0:T(8,128)(2,1)} async-done(((bf16[16,96,1024]{2,1,0:T(8,128)(2,1)}), bf16[16,96,1024]{2,1,0:T(8,128)(2,1)}, u32[]{:S(2)}, u32[]{:S(2)}) %all-to-all-start.1) | async-done | bytes 3145760 | tf_op jit(solution)/shard_map/all_to_all | solution.py:50
  195.1 2.6 convert_reduce_fusion.1
  197.7 0.1 multiply_convert_fusion
  197.8 0.4 stack.2
  198.2 0.0 copy-start.2
  198.2 79.5 %all_to_all.34 = bf16[16,96,1024]{2,1,0:T(8,128)(2,1)S(1)} all-to-all(bf16[16,96,1024]{2,1,0:T(8,128)(2,1)S(1)} %stack.2), channel_id=1, replica_groups=mesh['expert'=32,'tensor'=16] {'tensor'}, dimensions={0} | all-to-all | bytes 6291456 | tf_op jit(solution)/shard_map/all_to_all | solution.py:13
  277.7 0.0 copy-done.2
  277.7 3.2 fusion.1
  280.9 21.0 %all-to-all-start.4 = ((f32[32,48,384]{2,1,0:T(8,128)}), f32[32,48,384]{2,1,0:T(8,128)S(1)}, u32[]{:S(2)}, u32[]{:S(2)}) async-start(f32[32,48,384]{2,1,0:T(8,128)} %fusion.1), calls=%async_computation.4 | async-start | bytes 4718592 | tf_op jit(solution)/shard_map/all_to_all | solution.py:64
  301.9 55.5 %all-to-all-done.4 = f32[32,48,384]{2,1,0:T(8,128)S(1)} async-done(((f32[32,48,384]{2,1,0:T(8,128)}), f32[32,48,384]{2,1,0:T(8,128)S(1)}, u32[]{:S(2)}, u32[]{:S(2)}) %all-to-all-start.4) | async-done | bytes 2359328 | tf_op jit(solution)/shard_map/all_to_all | solution.py:64
  357.4 0.1 reduce_sum.49
  357.6 1.1 fusion
  (3 shorter events, 0.0 us)
Async XLA Ops:
  0.0 44.0 %copy-start = (bf16[1,1024,384]{2,1,0:T(8,128)(2,1)S(1)}, bf16[1,1024,384]{2,1,0:T(8,128)(2,1)}, u32[]{:S(2)}) copy-start(bf16[1,1024,384]{2,1,0:T(8,128)(2,1)} %param.10) | copy-start | bytes 2359300
  47.5 11.9 %copy-start.1 = (bf16[1,1024,384]{2,1,0:T(8,128)(2,1)S(1)}, bf16[1,1024,384]{2,1,0:T(8,128)(2,1)}, u32[]{:S(2)}) copy-start(bf16[1,1024,384]{2,1,0:T(8,128)(2,1)} %param.9) | copy-start | bytes 2359300
  47.5 74.1 %all-to-all-start.2 = ((bf16[16,96,1024]{2,1,0:T(8,128)(2,1)}), bf16[16,96,1024]{2,1,0:T(8,128)(2,1)}, u32[]{:S(2)}, u32[]{:S(2)}) async-start(bf16[16,96,1024]{2,1,0:T(8,128)(2,1)} %bitcast.30), calls=%async_computation.2 | async-start | bytes 6291456 | tf_op jit(solution)/shard_map/all_to_all | solution.py:51
  121.6 73.5 %all-to-all-start.1 = ((bf16[16,96,1024]{2,1,0:T(8,128)(2,1)}), bf16[16,96,1024]{2,1,0:T(8,128)(2,1)}, u32[]{:S(2)}, u32[]{:S(2)}) async-start(bf16[16,96,1024]{2,1,0:T(8,128)(2,1)} %bitcast.29), calls=%async_computation.1 | async-start | bytes 6291456 | tf_op jit(solution)/shard_map/all_to_all | solution.py:50
  198.2 79.5 %copy-start.2 = (bf16[1,1024,384]{2,1,0:T(8,128)(2,1)S(1)}, bf16[1,1024,384]{2,1,0:T(8,128)(2,1)}, u32[]{:S(2)}) copy-start(bf16[1,1024,384]{2,1,0:T(8,128)(2,1)} %param.11) | copy-start | bytes 2359300
  280.9 76.5 %all-to-all-start.4 = ((f32[32,48,384]{2,1,0:T(8,128)}), f32[32,48,384]{2,1,0:T(8,128)S(1)}, u32[]{:S(2)}, u32[]{:S(2)}) async-start(f32[32,48,384]{2,1,0:T(8,128)} %fusion.1), calls=%async_computation.4 | async-start | bytes 4718592 | tf_op jit(solution)/shard_map/all_to_all | solution.py:64
